TPU v7x, 256 devices: a whole 4x4x8 slice. The times are simulated.
256 devices in a mesh: seq: 16 (over z_lo, y), head: 16 (over x, z_hi, core).
Axes of the slice: x: 4, y: 4, z: 8 (z_hi: 2, z_lo: 4; z = z_hi * 4 + z_lo), core: 2. Of those that a mesh axis runs over, the one named last changes fastest.
Arguments:
- query: bfloat16 [16384, 2048], P(('seq', 'head')), may hold values from -6 to 6
- key: bfloat16 [16384, 2048], P(('seq', 'head')), may hold values from -6 to 6
- value: bfloat16 [16384, 2048], P(('seq', 'head')), may hold values from -6 to 6
- output: bfloat16 [16384, 2048], P(('seq', 'head')), may hold values from -6 to 6
- grad_out: bfloat16 [16384, 2048], P(('seq', 'head')), may hold values from -6 to 6
- logsumexp: float32 [16, 16384], P('head', 'seq'), may hold values from 3.5 to 8.5, as said below
- rand_blocks: int32 [256, 3], replicated, may hold values from 0 to 255, as said below
Outputs:
- grad_query: bfloat16 [16384, 2048], P(('seq', 'head'))
- grad_key: bfloat16 [16384, 2048], P(('seq', 'head'))
- grad_value: bfloat16 [16384, 2048], P(('seq', 'head'))
Inputs may be any that keep to these rules, and one draw needn't show every extreme that they name: `rand_blocks`: each row names 3 different blocks, none below 2 and none within one block of the row's own block. In aligned runs of 16 rows, exactly 3 of the run's entries fall in each aligned run of 16 key blocks. `logsumexp`: rows of the first 2 blocks lie between 7 and 8.5, all others between 3.5 and 5.
All inputs are finite; a program needn't handle non-finite values.
Results may differ from a plain program's by a relative error of at most 0.02.
Values may be sent and summed in bfloat16 or wider, within the bound.
No kernel may reach another device: no remote copies, remote signals or barrier semaphores. Data moves between devices by JAX's collectives and lax.ppermute only.
A program may use at most 64 MiB of HBM per device.

v0:
```python
import jax
import jax.numpy as jnp
from jax import lax
from jax.sharding import PartitionSpec as P

HEADS = 16
HD = 128
BLK = 64
GLOB = 2
RAND = 3


def spread(value, axis, source):
    kept = jnp.where(lax.axis_index(axis) == source, value, 0).astype(value.dtype)
    return lax.psum(kept, axis)


def passed_along(value, axis, steps):
    count = lax.axis_size(axis)
    initial, last = (max(0, -steps), min(count, count - steps))
    return lax.ppermute(value, axis, [(source, source + steps) for source in range(initial, last)])


def block_grads(queries, grad_rows, log_norm, deltas, keys, values, usable, factor):
    scores = (
        jnp.einsum("...md,...nd->...mn", queries, keys, preferred_element_type=jnp.float32) * factor
    )
    weights = jnp.where(usable, jnp.exp(scores - log_norm[..., None]), 0.0)
    weights_low = weights.astype(jnp.bfloat16)
    grad_values = jnp.einsum(
        "...mn,...md->...nd", weights_low, grad_rows, preferred_element_type=jnp.float32
    )
    grad_probs = jnp.einsum(
        "...md,...nd->...mn", grad_rows, values, preferred_element_type=jnp.float32
    )
    grad_scores = (weights * (grad_probs - deltas[..., None])).astype(jnp.bfloat16)
    grad_queries = (
        jnp.einsum("...mn,...nd->...md", grad_scores, keys, preferred_element_type=jnp.float32)
        * factor
    )
    grad_keys = (
        jnp.einsum("...mn,...md->...nd", grad_scores, queries, preferred_element_type=jnp.float32)
        * factor
    )
    return (grad_queries, grad_keys, grad_values)


def slide_blocks(stack, offset):
    if offset == 0:
        return stack
    blank = jnp.zeros_like(stack[:, :1])
    if offset > 0:
        return jnp.concatenate([stack[:, 1:], blank], axis=1)
    return jnp.concatenate([blank, stack[:, :-1]], axis=1)


def slot_order(rand_blocks, group_id, blocks_here):
    pattern_rows = lax.dynamic_slice_in_dim(rand_blocks, group_id * blocks_here, blocks_here, 0)
    entries = pattern_rows.reshape(-1)
    ranking = jnp.argsort(entries // blocks_here, stable=True)
    slot_query = ranking // rand_blocks.shape[1]
    slot_key = entries[ranking] % blocks_here
    return (slot_query, slot_key)


def per_device(query, key, value, output, grad_out, logsumexp, rand_blocks):
    tok_rows = query.shape[0]
    heads_here = logsumexp.shape[0]
    seq_rows = logsumexp.shape[1]
    blocks_here = seq_rows // BLK
    groups = lax.axis_size("seq")
    position = lax.axis_index("seq")
    per_group = RAND * blocks_here // groups
    glob_rows = GLOB * BLK
    factor = HD ** (-0.5)

    def to_heads(matrix):
        return matrix.reshape(tok_rows, HEADS, HD).transpose(1, 0, 2)

    query_rows, key_rows, value_rows, out_rows, grad_rows = (
        lax.all_to_all(to_heads(query), "head", split_axis=0, concat_axis=1, tiled=True),
        lax.all_to_all(to_heads(key), "head", split_axis=0, concat_axis=1, tiled=True),
        lax.all_to_all(to_heads(value), "head", split_axis=0, concat_axis=1, tiled=True),
        lax.all_to_all(to_heads(output), "head", split_axis=0, concat_axis=1, tiled=True),
        lax.all_to_all(to_heads(grad_out), "head", split_axis=0, concat_axis=1, tiled=True),
    )
    deltas = jnp.sum(grad_rows.astype(jnp.float32) * out_rows.astype(jnp.float32), axis=-1)

    def as_blocks(stack):
        return stack.reshape((heads_here, blocks_here, BLK) + stack.shape[2:])

    query_blk = as_blocks(query_rows)
    key_blk = as_blocks(key_rows)
    value_blk = as_blocks(value_rows)
    grad_blk = as_blocks(grad_rows)
    norm_blk = as_blocks(logsumexp)
    delta_blk = as_blocks(deltas)
    block_ids = jnp.arange(blocks_here, dtype=jnp.int32)
    first_id = position * blocks_here
    query_alive = first_id + block_ids >= GLOB
    grad_query = jnp.zeros((heads_here, blocks_here, BLK, HD), jnp.float32)
    grad_key_home = jnp.zeros_like(grad_query)
    grad_value_home = jnp.zeros_like(grad_query)
    for offset in (-1, 0, 1):
        target = block_ids + offset
        usable = query_alive & (target >= 0) & (target < blocks_here) & (first_id + target >= GLOB)
        part_q, part_k, part_v = block_grads(
            query_blk,
            grad_blk,
            norm_blk,
            delta_blk,
            slide_blocks(key_blk, offset),
            slide_blocks(value_blk, offset),
            usable[None, :, None, None],
            factor,
        )
        grad_query = grad_query + part_q
        grad_key_home = grad_key_home + slide_blocks(part_k, -offset)
        grad_value_home = grad_value_home + slide_blocks(part_v, -offset)
    row_alive = jnp.repeat(query_alive, BLK)
    at_home = (position == 0).astype(jnp.float32)
    glob_key, glob_value, glob_query, glob_grad = (
        spread(key_rows[:, :glob_rows], "seq", 0),
        spread(value_rows[:, :glob_rows], "seq", 0),
        spread(query_rows[:, :glob_rows], "seq", 0),
        spread(grad_rows[:, :glob_rows], "seq", 0),
    )
    glob_norm, glob_delta = (
        spread(logsumexp[:, :glob_rows], "seq", 0),
        spread(deltas[:, :glob_rows], "seq", 0),
    )
    key_part_q, key_part_k, key_part_v = block_grads(
        query_rows,
        grad_rows,
        logsumexp,
        deltas,
        glob_key,
        glob_value,
        row_alive[None, :, None],
        factor,
    )
    grad_query = grad_query + as_blocks(key_part_q)
    spread_q, spread_k, spread_v = block_grads(
        glob_query, glob_grad, glob_norm, glob_delta, key_rows, value_rows, True, factor
    )
    grad_key_home = grad_key_home + as_blocks(spread_k)
    grad_value_home = grad_value_home + as_blocks(spread_v)
    totals_k, totals_v, totals_q = (
        lax.psum(key_part_k.astype(jnp.bfloat16), "seq").astype(jnp.float32),
        lax.psum(key_part_v.astype(jnp.bfloat16), "seq").astype(jnp.float32),
        lax.psum(spread_q.astype(jnp.bfloat16), "seq").astype(jnp.float32),
    )
    grad_query = grad_query.at[:, :GLOB].add(at_home * totals_q.reshape(heads_here, GLOB, BLK, HD))
    grad_key_home = grad_key_home.at[:, :GLOB].add(
        at_home * totals_k.reshape(heads_here, GLOB, BLK, HD)
    )
    grad_value_home = grad_value_home.at[:, :GLOB].add(
        at_home * totals_v.reshape(heads_here, GLOB, BLK, HD)
    )
    slot_q = slot_order(rand_blocks, position, blocks_here)[0]

    def wanted(anchor):
        return slot_order(rand_blocks, anchor, blocks_here)[1]

    all_wanted = jax.vmap(wanted)(jnp.arange(groups, dtype=jnp.int32))
    send_ids = lax.dynamic_slice_in_dim(all_wanted, position * per_group, per_group, 1).reshape(-1)
    far_key, far_value = (
        lax.all_to_all(key_blk[:, send_ids], "seq", split_axis=1, concat_axis=1, tiled=True),
        lax.all_to_all(value_blk[:, send_ids], "seq", split_axis=1, concat_axis=1, tiled=True),
    )
    usable = first_id + slot_q >= GLOB
    part_q, part_k, part_v = block_grads(
        query_blk[:, slot_q],
        grad_blk[:, slot_q],
        norm_blk[:, slot_q],
        delta_blk[:, slot_q],
        far_key,
        far_value,
        usable[None, :, None, None],
        factor,
    )
    grad_query = grad_query.at[:, slot_q].add(part_q)
    back_key, back_value = (
        lax.all_to_all(part_k, "seq", split_axis=1, concat_axis=1, tiled=True),
        lax.all_to_all(part_v, "seq", split_axis=1, concat_axis=1, tiled=True),
    )
    grad_key_home = grad_key_home.at[:, send_ids].add(back_key)
    grad_value_home = grad_value_home.at[:, send_ids].add(back_value)
    left_key, left_value = passed_along((key_blk[:, -1:], value_blk[:, -1:]), "seq", 1)
    right_key, right_value = passed_along((key_blk[:, :1], value_blk[:, :1]), "seq", -1)
    left_ok = (position >= 1) & (first_id - 1 >= GLOB)
    right_ok = (position <= groups - 2) & (first_id + blocks_here - 1 >= GLOB)
    left_q, left_k, left_v = block_grads(
        query_blk[:, :1],
        grad_blk[:, :1],
        norm_blk[:, :1],
        delta_blk[:, :1],
        left_key,
        left_value,
        left_ok,
        factor,
    )
    right_q, right_k, right_v = block_grads(
        query_blk[:, -1:],
        grad_blk[:, -1:],
        norm_blk[:, -1:],
        delta_blk[:, -1:],
        right_key,
        right_value,
        right_ok,
        factor,
    )
    grad_query = grad_query.at[:, :1].add(left_q)
    grad_query = grad_query.at[:, -1:].add(right_q)
    from_right_k, from_right_v = (
        passed_along(left_k.astype(jnp.bfloat16), "seq", -1).astype(left_k.dtype),
        passed_along(left_v.astype(jnp.bfloat16), "seq", -1).astype(left_v.dtype),
    )
    from_left_k, from_left_v = (
        passed_along(right_k.astype(jnp.bfloat16), "seq", 1).astype(right_k.dtype),
        passed_along(right_v.astype(jnp.bfloat16), "seq", 1).astype(right_v.dtype),
    )
    grad_key_home = grad_key_home.at[:, -1:].add(from_right_k)
    grad_value_home = grad_value_home.at[:, -1:].add(from_right_v)
    grad_key_home = grad_key_home.at[:, :1].add(from_left_k)
    grad_value_home = grad_value_home.at[:, :1].add(from_left_v)

    def to_rows(stack):
        return stack.astype(jnp.bfloat16).reshape(heads_here, seq_rows, HD)

    back_q, back_k, back_v = (
        lax.all_to_all(to_rows(grad_query), "head", split_axis=1, concat_axis=0, tiled=True),
        lax.all_to_all(to_rows(grad_key_home), "head", split_axis=1, concat_axis=0, tiled=True),
        lax.all_to_all(to_rows(grad_value_home), "head", split_axis=1, concat_axis=0, tiled=True),
    )

    def to_tokens(stack):
        return stack.transpose(1, 0, 2).reshape(tok_rows, HEADS * HD)

    return (to_tokens(back_q), to_tokens(back_k), to_tokens(back_v))


def solution(mesh):
    in_specs = (
        P(("seq", "head"), None),
        P(("seq", "head"), None),
        P(("seq", "head"), None),
        P(("seq", "head"), None),
        P(("seq", "head"), None),
        P("head", "seq"),
        P(),
    )
    out_specs = (P(("seq", "head"), None), P(("seq", "head"), None), P(("seq", "head"), None))
    return jax.shard_map(
        per_device, mesh=mesh, in_specs=in_specs, out_specs=out_specs, check_vma=False
    )
```

profile of v0, /device:TPU:64, one launch (start us, length us, event | category | flops | bytes accessed | tf_op | source)
XLA Modules:
  0.0 658.4 jit_solution(3117383005306899725)
XLA Ops:
  8.9 9.2 %all-to-all-start = ((bf16[16,64,128]{2,1,0:T(8,128)(2,1)}), bf16[16,64,128]{2,1,0:T(8,128)(2,1)S(1)}, u32[]{:S(2)}, u32[]{:S(2)}) async-start(bf16[16,64,128]{2,1,0:T(8,128)(2,1)} %bitcast_bitcast_fusion.4), calls=%async_computation | async-start | bytes 524288 | tf_op jit(solution)/shard_map/all_to_all | solution.py:82
  18.2 32.0 %while.10 = (s32[]{:T(128)}, s32[256,3]{0,1:T(4,128)}, s32[16,2]{0,1:T(2,128)S(1)}, s32[16,16,3]{1,2,0:T(4,128)S(1)}, s32[]{:T(128)}) while((s32[]{:T(128)}, s32[256,3]{0,1:T(4,128)}, s32[16,2]{0,1:T(2,128)S(1)}, s32[16,16,3]{1,2,0:T(4,128)S(1)}, s32[]{:T(128)}) %tuple.65), condition=%wide.while_cond.9, body=%wide.while_body.9.sunk | while | flops 2 | bytes 2345 | solution.py:58
  51.5 5.3 gather_fusion.6
  61.6 9.6 %all-to-all-start.2 = ((bf16[16,64,128]{2,1,0:T(8,128)(2,1)}), bf16[16,64,128]{2,1,0:T(8,128)(2,1)S(1)}, u32[]{:S(2)}, u32[]{:S(2)}) async-start(bf16[16,64,128]{2,1,0:T(8,128)(2,1)} %bitcast_bitcast_fusion.2), calls=%async_computation.2 | async-start | bytes 524288 | tf_op jit(solution)/shard_map/all_to_all | solution.py:83
  72.1 13.9 %all-to-all-done.2 = bf16[16,64,128]{2,1,0:T(8,128)(2,1)S(1)} async-done(((bf16[16,64,128]{2,1,0:T(8,128)(2,1)}), bf16[16,64,128]{2,1,0:T(8,128)(2,1)S(1)}, u32[]{:S(2)}, u32[]{:S(2)}) %all-to-all-start.2) | async-done | bytes 262176 | tf_op jit(solution)/shard_map/all_to_all | solution.py:83
  86.0 3.5 all-to-all-start.4
  91.6 10.8 %all-to-all-done.4 = bf16[16,64,128]{2,1,0:T(8,128)(2,1)S(1)} async-done(((bf16[16,64,128]{2,1,0:T(8,128)(2,1)}), bf16[16,64,128]{2,1,0:T(8,128)(2,1)S(1)}, u32[]{:S(2)}, u32[]{:S(2)}) %all-to-all-start.4) | async-done | bytes 262176 | tf_op jit(solution)/shard_map/all_to_all | solution.py:84
  102.4 3.5 all-to-all-start.3
  109.1 8.8 %all-to-all-done.3 = bf16[16,64,128]{2,1,0:T(8,128)(2,1)S(1)} async-done(((bf16[16,64,128]{2,1,0:T(8,128)(2,1)}), bf16[16,64,128]{2,1,0:T(8,128)(2,1)S(1)}, u32[]{:S(2)}, u32[]{:S(2)}) %all-to-all-start.3) | async-done | bytes 262176 | tf_op jit(solution)/shard_map/all_to_all | solution.py:85
  118.0 3.5 all-to-all-start.1
  124.0 9.5 %all-to-all-done.1 = bf16[16,64,128]{2,1,0:T(8,128)(2,1)S(1)} async-done(((bf16[16,64,128]{2,1,0:T(8,128)(2,1)}), bf16[16,64,128]{2,1,0:T(8,128)(2,1)S(1)}, u32[]{:S(2)}, u32[]{:S(2)}) %all-to-all-start.1) | async-done | bytes 262176 | tf_op jit(solution)/shard_map/all_to_all | solution.py:81
  134.7 5.4 collective-permute-start.2
  142.6 6.0 collective-permute-start.3
  155.6 7.3 %all-to-all-start.5 = ((bf16[1,48,64,128]{3,2,0,1:T(8,128)(2,1)}), bf16[1,48,64,128]{3,2,0,1:T(8,128)(2,1)S(1)}, u32[]{:S(2)}, u32[]{:S(2)}) async-start(bf16[1,48,64,128]{3,2,0,1:T(8,128)(2,1)} %bitcast.32), calls=%async_computation.5 | async-start | bytes 1572864 | tf_op jit(solution)/shard_map/all_to_all | solution.py:168
  170.5 36.8 %all-reduce.9 = (f32[128]{0:T(128)}, f32[128]{0:T(128)S(1)}) all-reduce(f32[128]{0:T(128)S(1)} %copy-done.53, f32[128]{0:T(128)S(1)} %copy-done.54), channel_id=1, replica_groups=mesh['seq'=16,'head'=16] {'seq'}, use_global_device_ids=true, to_apply=%region_4.5 | all-reduce | flops 256 | bytes 2048 | tf_op jit(solution)/shard_map/psum | solution.py:15
  207.8 107.8 %all-reduce.17.cloned.1.call-done = (bf16[128,128]{1,0:T(8,128)(2,1)}, bf16[128,128]{1,0:T(8,128)(2,1)}, bf16[128,128]{1,0:T(8,128)(2,1)}, bf16[128,128]{1,0:T(8,128)(2,1)}) async-done(((bf16[128,128]{1,0:T(8,128)(2,1)}, bf16[128,128]{1,0:T(8,128)(2,1)}, bf16[128,128]{1,0:T(8,128)(2,1)}, bf16[128,128]{1,0:T(8,128)(2,1)}), (bf16[128,128]{1,0:T(8,128)(2,1)}, bf16[128,128]{1,0:T(8,128)(2,1)}, ...) | async-done | bytes 131088 | tf_op jit(solution)/shard_map/psum | solution.py:15
  320.6 14.9 %all-to-all-start.6 = ((bf16[1,48,64,128]{3,2,0,1:T(8,128)(2,1)}), bf16[1,48,64,128]{3,2,0,1:T(8,128)(2,1)}, u32[]{:S(2)}, u32[]{:S(2)}) async-start(bf16[1,48,64,128]{3,2,0,1:T(8,128)(2,1)} %bitcast.35), calls=%async_computation.6 | async-start | bytes 1572864 | tf_op jit(solution)/shard_map/all_to_all | solution.py:169
  340.1 144.8 %all-reduce.15.cloned.1.call-done = (bf16[1,128,128]{2,1,0:T(8,128)(2,1)}, bf16[1,128,128]{2,1,0:T(8,128)(2,1)}, bf16[1,128,128]{2,1,0:T(8,128)(2,1)}) async-done(((bf16[1,128,128]{2,1,0:T(8,128)(2,1)}, bf16[1,128,128]{2,1,0:T(8,128)(2,1)}, bf16[1,128,128]{2,1,0:T(8,128)(2,1)}), (bf16[1,128,128]{2,1,0:T(8,128)(2,1)}, bf16[1,128,128]{2,1,0:T(8,128)(2,1)}, ...) | async-done | bytes 98320 | tf_op jit(solution)/shard_map/psum | solution.py:151
  492.5 5.4 scatter_fusion
  502.0 8.2 %all-to-all-start.7 = ((bf16[16,2,4096]{2,1,0:T(2,128)(2,1)}), bf16[16,2,4096]{2,1,0:T(2,128)(2,1)S(1)}, u32[]{:S(2)}, u32[]{:S(2)}) async-start(bf16[16,2,4096]{2,1,0:T(2,128)(2,1)} %reshape.1100), calls=%async_computation.7 | async-start | bytes 524288 | tf_op jit(solution)/shard_map/all_to_all | solution.py:232
  513.3 9.0 %all-to-all-done.7 = bf16[16,2,4096]{2,1,0:T(2,128)(2,1)S(1)} async-done(((bf16[16,2,4096]{2,1,0:T(2,128)(2,1)}), bf16[16,2,4096]{2,1,0:T(2,128)(2,1)S(1)}, u32[]{:S(2)}, u32[]{:S(2)}) %all-to-all-start.7) | async-done | bytes 262176 | tf_op jit(solution)/shard_map/all_to_all | solution.py:232
  522.3 11.6 %all-to-all-start.10 = ((f32[1,48,64,128]{3,2,0,1:T(8,128)}), f32[1,48,64,128]{3,2,0,1:T(8,128)}, u32[]{:S(2)}, u32[]{:S(2)}) async-start(f32[1,48,64,128]{3,2,0,1:T(8,128)} %convolution_bitcast_fusion), calls=%async_computation.10 | async-start | bytes 3145728 | tf_op jit(solution)/shard_map/all_to_all | solution.py:185
  535.5 35.5 %all-to-all-done.10 = f32[1,48,64,128]{3,2,0,1:T(8,128)} async-done(((f32[1,48,64,128]{3,2,0,1:T(8,128)}), f32[1,48,64,128]{3,2,0,1:T(8,128)}, u32[]{:S(2)}, u32[]{:S(2)}) %all-to-all-start.10) | async-done | bytes 1572896 | tf_op jit(solution)/shard_map/all_to_all | solution.py:185
  571.0 5.1 all-to-all-start.8
  578.9 3.5 collective-permute-start.5
  582.6 4.6 collective-permute-start.4
  600.6 5.4 scatter_fusion.2
  606.0 3.5 collective-permute-done.6
  616.8 4.2 all-to-all-start.11
  628.9 4.0 all-to-all-done.11
  632.9 5.6 all-to-all-start.9
  640.7 9.8 %all-to-all-done.9 = bf16[16,2,4096]{2,1,0:T(2,128)(2,1)S(1)} async-done(((bf16[16,2,4096]{2,1,0:T(2,128)(2,1)}), bf16[16,2,4096]{2,1,0:T(2,128)(2,1)S(1)}, u32[]{:S(2)}, u32[]{:S(2)}) %all-to-all-start.9) | async-done | bytes 262176 | tf_op jit(solution)/shard_map/all_to_all | solution.py:233
  (325 shorter events, 127.0 us)
Async XLA Ops:
  8.9 52.7 %all-to-all-start = ((bf16[16,64,128]{2,1,0:T(8,128)(2,1)}), bf16[16,64,128]{2,1,0:T(8,128)(2,1)S(1)}, u32[]{:S(2)}, u32[]{:S(2)}) async-start(bf16[16,64,128]{2,1,0:T(8,128)(2,1)} %bitcast_bitcast_fusion.4), calls=%async_computation | async-start | bytes 524288 | tf_op jit(solution)/shard_map/all_to_all | solution.py:82
  56.8 33.2 %copy-start.29 = (bf16[64,2048]{1,0:T(8,128)(2,1)S(1)}, bf16[64,2048]{1,0:T(8,128)(2,1)}, u32[]{:S(2)}) copy-start(bf16[64,2048]{1,0:T(8,128)(2,1)} %param.25) | copy-start | bytes 786436
  56.9 34.0 %copy-start.30 = (bf16[64,2048]{1,0:T(8,128)(2,1)S(1)}, bf16[64,2048]{1,0:T(8,128)(2,1)}, u32[]{:S(2)}) copy-start(bf16[64,2048]{1,0:T(8,128)(2,1)} %param.29) | copy-start | bytes 786436
  61.6 24.4 %all-to-all-start.2 = ((bf16[16,64,128]{2,1,0:T(8,128)(2,1)}), bf16[16,64,128]{2,1,0:T(8,128)(2,1)S(1)}, u32[]{:S(2)}, u32[]{:S(2)}) async-start(bf16[16,64,128]{2,1,0:T(8,128)(2,1)} %bitcast_bitcast_fusion.2), calls=%async_computation.2 | async-start | bytes 524288 | tf_op jit(solution)/shard_map/all_to_all | solution.py:83
  86.0 16.4 %all-to-all-start.4 = ((bf16[16,64,128]{2,1,0:T(8,128)(2,1)}), bf16[16,64,128]{2,1,0:T(8,128)(2,1)S(1)}, u32[]{:S(2)}, u32[]{:S(2)}) async-start(bf16[16,64,128]{2,1,0:T(8,128)(2,1)} %bitcast_bitcast_fusion), calls=%async_computation.4 | async-start | bytes 524288 | tf_op jit(solution)/shard_map/all_to_all | solution.py:84
  102.4 15.6 %all-to-all-start.3 = ((bf16[16,64,128]{2,1,0:T(8,128)(2,1)}), bf16[16,64,128]{2,1,0:T(8,128)(2,1)S(1)}, u32[]{:S(2)}, u32[]{:S(2)}) async-start(bf16[16,64,128]{2,1,0:T(8,128)(2,1)} %bitcast_bitcast_fusion.1), calls=%async_computation.3 | async-start | bytes 524288 | tf_op jit(solution)/shard_map/all_to_all | solution.py:85
  118.0 15.5 %all-to-all-start.1 = ((bf16[16,64,128]{2,1,0:T(8,128)(2,1)}), bf16[16,64,128]{2,1,0:T(8,128)(2,1)S(1)}, u32[]{:S(2)}, u32[]{:S(2)}) async-start(bf16[16,64,128]{2,1,0:T(8,128)(2,1)} %bitcast_bitcast_fusion.3), calls=%async_computation.1 | async-start | bytes 524288 | tf_op jit(solution)/shard_map/all_to_all | solution.py:81
  134.7 72.6 %collective-permute-start.2 = (bf16[1,1,64,128]{3,2,1,0:T(8,128)(2,1)S(1)}, bf16[1,1,64,128]{3,2,1,0:T(8,128)(2,1)S(1)}, u32[]{:S(2)}, u32[]{:S(2)}) collective-permute-start(bf16[1,1,64,128]{3,2,1,0:T(8,128)(2,1)S(1)} %get-tuple-element.144), channel_id=1, source_target_pairs={{16,0},{32,16},{48,32},{64,48},{80,64},{96,80},{112,96},{128,112},... | collective-permute-start | bytes 49160 | tf_op jit(solution)/shard_map/ppermute | solution.py:21
  140.1 67.4 %collective-permute-start = (bf16[1,1,64,128]{3,2,1,0:T(8,128)(2,1)S(1)}, bf16[1,1,64,128]{3,2,1,0:T(8,128)(2,1)S(1)}, u32[]{:S(2)}, u32[]{:S(2)}) collective-permute-start(bf16[1,1,64,128]{3,2,1,0:T(8,128)(2,1)S(1)} %get-tuple-element.145), channel_id=1, source_target_pairs={{0,16},{16,32},{32,48},{48,64},{64,80},{80,96},{96,112},{112,128},... | collective-permute-start | bytes 49160 | tf_op jit(solution)/shard_map/ppermute | solution.py:21
  142.6 64.8 %collective-permute-start.3 = (bf16[1,1,64,128]{3,2,1,0:T(8,128)(2,1)S(1)}, bf16[1,1,64,128]{3,2,1,0:T(8,128)(2,1)S(1)}, u32[]{:S(2)}, u32[]{:S(2)}) collective-permute-start(bf16[1,1,64,128]{3,2,1,0:T(8,128)(2,1)S(1)} %get-tuple-element.142), channel_id=1, source_target_pairs={{16,0},{32,16},{48,32},{64,48},{80,64},{96,80},{112,96},{128,112},... | collective-permute-start | bytes 49160 | tf_op jit(solution)/shard_map/ppermute | solution.py:21
  148.7 59.1 %collective-permute-start.1 = (bf16[1,1,64,128]{3,2,1,0:T(8,128)(2,1)S(1)}, bf16[1,1,64,128]{3,2,1,0:T(8,128)(2,1)S(1)}, u32[]{:S(2)}, u32[]{:S(2)}) collective-permute-start(bf16[1,1,64,128]{3,2,1,0:T(8,128)(2,1)S(1)} %get-tuple-element.143), channel_id=1, source_target_pairs={{0,16},{16,32},{32,48},{48,64},{64,80},{80,96},{96,112},{112,128},... | collective-permute-start | bytes 49160 | tf_op jit(solution)/shard_map/ppermute | solution.py:21
  155.6 165.0 %all-to-all-start.5 = ((bf16[1,48,64,128]{3,2,0,1:T(8,128)(2,1)}), bf16[1,48,64,128]{3,2,0,1:T(8,128)(2,1)S(1)}, u32[]{:S(2)}, u32[]{:S(2)}) async-start(bf16[1,48,64,128]{3,2,0,1:T(8,128)(2,1)} %bitcast.32), calls=%async_computation.5 | async-start | bytes 1572864 | tf_op jit(solution)/shard_map/all_to_all | solution.py:168
  163.0 152.7 %all-reduce.17.cloned.1.call-start = ((), (), s32[]{:S(2)}) async-start(), calls=%async_computation.13 | async-start | bytes 262144 | tf_op jit(solution)/shard_map/psum | solution.py:15
  168.9 146.7 %copy-start.48 = (pred[1024]{0:T(1024)(128)(4,1)S(1)}, pred[1024]{0:T(1024)(128)(4,1)}, u32[]{:S(2)}) copy-start(pred[1024]{0:T(1024)(128)(4,1)} %broadcast_in_dim.110) | copy-start | bytes 3076
  207.4 108.2 %copy-start.34 = (f32[64,64]{1,0:T(8,128)}, f32[64,64]{1,0:T(8,128)S(1)}, u32[]{:S(2)}) copy-start(f32[64,64]{1,0:T(8,128)S(1)} %fusion.41) | copy-start | bytes 49156
  207.5 111.3 %copy-start.44 = (bf16[1,1,64,128]{3,2,1,0:T(8,128)(2,1)}, bf16[1,1,64,128]{3,2,1,0:T(8,128)(2,1)S(1)}, u32[]{:S(2)}) copy-start(bf16[1,1,64,128]{3,2,1,0:T(8,128)(2,1)S(1)} %collective-permute-done) | copy-start | bytes 49156
  207.7 107.9 %copy-start.36 = (f32[64,64]{1,0:T(8,128)}, f32[64,64]{1,0:T(8,128)S(1)}, u32[]{:S(2)}) copy-start(f32[64,64]{1,0:T(8,128)S(1)} %fusion.46) | copy-start | bytes 49156
  320.6 168.0 %all-to-all-start.6 = ((bf16[1,48,64,128]{3,2,0,1:T(8,128)(2,1)}), bf16[1,48,64,128]{3,2,0,1:T(8,128)(2,1)}, u32[]{:S(2)}, u32[]{:S(2)}) async-start(bf16[1,48,64,128]{3,2,0,1:T(8,128)(2,1)} %bitcast.35), calls=%async_computation.6 | async-start | bytes 1572864 | tf_op jit(solution)/shard_map/all_to_all | solution.py:169
  335.5 149.4 %all-reduce.15.cloned.1.call-start = ((), (), s32[]{:S(2)}) async-start(), calls=%async_computation.12 | async-start | bytes 196608 | tf_op jit(solution)/shard_map/psum | solution.py:151
  337.4 148.3 %copy-start.3 = (bf16[48,64,128]{2,1,0:T(8,128)(2,1)S(1)}, bf16[48,64,128]{2,1,0:T(8,128)(2,1)}, u32[]{:S(2)}) copy-start(bf16[48,64,128]{2,1,0:T(8,128)(2,1)} %gather_fusion) | copy-start | bytes 2359300
  337.5 148.3 %copy-start.51 = (pred[48]{0:T(512)(128)(4,1)S(1)}, pred[48]{0:T(512)(128)(4,1)}, u32[]{:S(2)}) copy-start(pred[48]{0:T(512)(128)(4,1)} %get-tuple-element.140) | copy-start | bytes 148
  338.7 147.0 %copy-start.43 = (f32[48,64]{1,0:T(8,128)S(1)}, f32[48,64]{1,0:T(8,128)}, u32[]{:S(2)}) copy-start(f32[48,64]{1,0:T(8,128)} %gather_fusion.2) | copy-start | bytes 36868
  502.0 20.3 %all-to-all-start.7 = ((bf16[16,2,4096]{2,1,0:T(2,128)(2,1)}), bf16[16,2,4096]{2,1,0:T(2,128)(2,1)S(1)}, u32[]{:S(2)}, u32[]{:S(2)}) async-start(bf16[16,2,4096]{2,1,0:T(2,128)(2,1)} %reshape.1100), calls=%async_computation.7 | async-start | bytes 524288 | tf_op jit(solution)/shard_map/all_to_all | solution.py:232
  522.3 48.7 %all-to-all-start.10 = ((f32[1,48,64,128]{3,2,0,1:T(8,128)}), f32[1,48,64,128]{3,2,0,1:T(8,128)}, u32[]{:S(2)}, u32[]{:S(2)}) async-start(f32[1,48,64,128]{3,2,0,1:T(8,128)} %convolution_bitcast_fusion), calls=%async_computation.10 | async-start | bytes 3145728 | tf_op jit(solution)/shard_map/all_to_all | solution.py:185
  535.5 40.6 %copy-start.20 = (f32[16,64,64]{2,1,0:T(8,128)S(1)}, f32[16,64,64]{2,1,0:T(8,128)}, u32[]{:S(2)}) copy-start(f32[16,64,64]{2,1,0:T(8,128)} %copy-done.19) | copy-start | bytes 786436
  571.0 45.8 %all-to-all-start.8 = ((f32[1,48,64,128]{3,2,0,1:T(8,128)}), f32[1,48,64,128]{3,2,0,1:T(8,128)S(1)}, u32[]{:S(2)}, u32[]{:S(2)}) async-start(f32[1,48,64,128]{3,2,0,1:T(8,128)} %multiply_bitcast_fusion), calls=%async_computation.8 | async-start | bytes 3145728 | tf_op jit(solution)/shard_map/all_to_all | solution.py:184
  578.9 46.6 %collective-permute-start.5 = (bf16[1,1,64,128]{3,2,1,0:T(8,128)(2,1)S(1)}, bf16[1,1,64,128]{3,2,1,0:T(8,128)(2,1)S(1)}, u32[]{:S(2)}, u32[]{:S(2)}) collective-permute-start(bf16[1,1,64,128]{3,2,1,0:T(8,128)(2,1)S(1)} %fusion.58), channel_id=1, source_target_pairs={{0,16},{16,32},{32,48},{48,64},{64,80},{80,96},{96,112},{112,128},... | collective-permute-start | bytes 49160 | tf_op jit(solution)/shard_map/ppermute | solution.py:21
  582.6 42.2 %collective-permute-start.4 = (bf16[1,1,64,128]{3,2,1,0:T(8,128)(2,1)S(1)}, bf16[1,1,64,128]{3,2,1,0:T(8,128)(2,1)}, u32[]{:S(2)}, u32[]{:S(2)}) collective-permute-start(bf16[1,1,64,128]{3,2,1,0:T(8,128)(2,1)S(1)} %fusion.59), channel_id=1, source_target_pairs={{16,0},{32,16},{48,32},{64,48},{80,64},{96,80},{112,96},{128,112},... | collective-permute-start | bytes 49160 | tf_op jit(solution)/shard_map/ppermute | solution.py:21
  588.0 21.5 %collective-permute-start.6 = (bf16[1,1,64,128]{3,2,1,0:T(8,128)(2,1)}, bf16[1,1,64,128]{3,2,1,0:T(8,128)(2,1)}, u32[]{:S(2)}, u32[]{:S(2)}) collective-permute-start(bf16[1,1,64,128]{3,2,1,0:T(8,128)(2,1)} %fusion.56), channel_id=1, source_target_pairs={{16,0},{32,16},{48,32},{64,48},{80,64},{96,80},{112,96},{128,112},... | collective-permute-start | bytes 49160 | tf_op jit(solution)/shard_map/ppermute | solution.py:21
  591.2 21.5 %collective-permute-start.7 = (bf16[1,1,64,128]{3,2,1,0:T(8,128)(2,1)}, bf16[1,1,64,128]{3,2,1,0:T(8,128)(2,1)}, u32[]{:S(2)}, u32[]{:S(2)}) collective-permute-start(bf16[1,1,64,128]{3,2,1,0:T(8,128)(2,1)} %fusion.57), channel_id=1, source_target_pairs={{0,16},{16,32},{32,48},{48,64},{64,80},{80,96},{96,112},{112,128},... | collective-permute-start | bytes 49160 | tf_op jit(solution)/shard_map/ppermute | solution.py:21
  616.8 16.1 %all-to-all-start.11 = ((bf16[16,2,4096]{2,1,0:T(2,128)(2,1)}), bf16[16,2,4096]{2,1,0:T(2,128)(2,1)S(1)}, u32[]{:S(2)}, u32[]{:S(2)}) async-start(bf16[16,2,4096]{2,1,0:T(2,128)(2,1)} %reshape.1104), calls=%async_computation.11 | async-start | bytes 524288 | tf_op jit(solution)/shard_map/all_to_all | solution.py:234
  632.9 17.5 %all-to-all-start.9 = ((bf16[16,2,4096]{2,1,0:T(2,128)(2,1)}), bf16[16,2,4096]{2,1,0:T(2,128)(2,1)S(1)}, u32[]{:S(2)}, u32[]{:S(2)}) async-start(bf16[16,2,4096]{2,1,0:T(2,128)(2,1)} %reshape.1102), calls=%async_computation.9 | async-start | bytes 524288 | tf_op jit(solution)/shard_map/all_to_all | solution.py:233
  (48 other events, 297.6 us)
Sparse Core Ops, SparseCore 0:
  167.2 148.3 all-reduce.16
  339.4 145.4 all-reduce.14
where the time goes:
time: 661 us; the launch traced here: 658 us
  waiting for transfers between devices  361 us (55%)
  starting transfers between devices  116 us (18%)
  local copies, waits for them, and re-layouts  67.5 us (10%)
  blocking collectives  36.8 us (6%)
  other arithmetic  33.5 us (5%)
  matrix products  28.9 us (4%)
  between operations  15.3 us (2%)
    psum x1, waiting for transfers between devices, per_device(): lax.psum(spread_q.astype(jnp.bfloat16), 'seq').astype(jnp.float32)  145 us
    psum x1, waiting for transfers between devices, spread(): return lax.psum(kept, axis)  108 us
    psum x1, blocking collectives, spread(): return lax.psum(kept, axis)  36.8 us
    all_to_all x1, waiting for transfers between devices, per_device(): lax.all_to_all(part_v, 'seq', split_axis=1, concat_axis=1, tiled=True)  35.5 us
    gather x48, local copies, waits for them, and re-layouts  32 us
    ppermute x8, starting transfers between devices, passed_along(): lax.ppermute(value, axis, [(source, source + steps) for source in range(i...  29.1 us
    all_to_all x1, starting transfers between devices, per_device(): lax.all_to_all(value_blk[:, send_ids], 'seq', split_axis=1, concat_axis=1...  14.9 us
    all_to_all x1, waiting for transfers between devices, per_device(): lax.all_to_all(to_heads(value), 'head', split_axis=0, concat_axis=1, tile...  13.9 us
  transfers between devices with their start and end apart: 22, of which 12 were waited for; matrix products, arithmetic and copies ran while one was open for 16% of the time, Pallas kernels for 0%

commit v1 on v0

--- a/solution.py
+++ b/solution.py
@@ -230,7 +230,15 @@
 
     back_q, back_k, back_v = (
         lax.all_to_all(to_rows(grad_query), "head", split_axis=1, concat_axis=0, tiled=True),
-        lax.all_to_all(to_rows(grad_key_home), "head", split_axis=1, concat_axis=0, tiled=True),
+        jnp.concatenate(
+            lax.all_to_all(
+                jnp.stack(jnp.split(to_rows(grad_key_home), lax.axis_size("head"), axis=1)),
+                "head",
+                0,
+                0,
+            ),
+            axis=0,
+        ),
         lax.all_to_all(to_rows(grad_value_home), "head", split_axis=1, concat_axis=0, tiled=True),
     )
 

time: 661 us -> 609 us (0.921)
  waiting for transfers between devices: 361 us -> 292 us
  local copies, waits for them, and re-layouts: 67.5 us -> 77.5 us
    all_to_all x1, waiting for transfers between devices: 35.5 us -> 4.7 us  [per_device(): lax.all_to_all(part_v, 'seq', split_axis=1, concat_axis=1, tiled=True)]
    psum x1, waiting for transfers between devices: 108 us -> 83 us  [spread(): return lax.psum(kept, axis)]
    all_to_all x1, starting transfers between devices: 5.1 us -> 14.7 us  [per_device(): lax.all_to_all(part_k, 'seq', split_axis=1, concat_axis=1, tiled=True)]
    unnamed x125 -> x133, local copies, waits for them, and re-layouts: 9.19 us -> 17.2 us
    all_to_all x1, waiting for transfers between devices: 9.02 us -> 1.19 us  [per_device(): lax.all_to_all(to_rows(grad_query), 'head', split_axis=1, concat_axis=0,...]
    all_to_all x1, waiting for transfers between devices: 4.05 us -> 11.4 us  [per_device(): lax.all_to_all(to_rows(grad_value_home), 'head', split_axis=1, concat_axi...]
  transfers between devices with their start and end apart: 22 -> 22, of which waited for: 12 -> 10; matrix products, arithmetic and copies ran while one was open for 16% -> 22% of each run, Pallas kernels for 0% -> 0%
where the time goes in v1:
time: 609 us; the launch traced here: 604 us
  waiting for transfers between devices  292 us (48%)
  starting transfers between devices  121 us (20%)
  local copies, waits for them, and re-layouts  77.5 us (13%)
  other arithmetic  36.8 us (6%)
  blocking collectives  34.8 us (6%)
  matrix products  27.1 us (4%)
  between operations  15.2 us (2%)
    psum x1, waiting for transfers between devices, per_device(): lax.psum(spread_q.astype(jnp.bfloat16), 'seq').astype(jnp.float32)  140 us
    psum x1, waiting for transfers between devices, spread(): return lax.psum(kept, axis)  83 us
    psum x1, blocking collectives, spread(): return lax.psum(kept, axis)  34.8 us
    gather x48, local copies, waits for them, and re-layouts  32 us
    ppermute x8, starting transfers between devices, passed_along(): lax.ppermute(value, axis, [(source, source + steps) for source in range(i...  29 us
    unnamed x133, local copies, waits for them, and re-layouts  17.2 us
    all_to_all x1, starting transfers between devices, per_device(): lax.all_to_all(part_k, 'seq', split_axis=1, concat_axis=1, tiled=True)  14.7 us
    all_to_all x1, waiting for transfers between devices, per_device(): lax.all_to_all(to_heads(value), 'head', split_axis=0, concat_axis=1, tile...  12.8 us
  transfers between devices with their start and end apart: 22, of which 10 were waited for; matrix products, arithmetic and copies ran while one was open for 22% of the time, Pallas kernels for 0%

profile of v1, /device:TPU:64, one launch (start us, length us, event | category | flops | bytes accessed | tf_op | source)
XLA Modules:
  0.0 604.3 jit_solution(11631536498174579379)
XLA Ops:
  8.9 9.2 %all-to-all-start = ((bf16[16,64,128]{2,1,0:T(8,128)(2,1)}), bf16[16,64,128]{2,1,0:T(8,128)(2,1)S(1)}, u32[]{:S(2)}, u32[]{:S(2)}) async-start(bf16[16,64,128]{2,1,0:T(8,128)(2,1)} %bitcast_bitcast_fusion.4), calls=%async_computation | async-start | bytes 524288 | tf_op jit(solution)/shard_map/all_to_all | solution.py:82
  18.2 32.0 %while.10 = (s32[]{:T(128)}, s32[256,3]{0,1:T(4,128)}, s32[16,2]{0,1:T(2,128)S(1)}, s32[16,16,3]{1,2,0:T(4,128)S(1)}, s32[]{:T(128)}) while((s32[]{:T(128)}, s32[256,3]{0,1:T(4,128)}, s32[16,2]{0,1:T(2,128)S(1)}, s32[16,16,3]{1,2,0:T(4,128)S(1)}, s32[]{:T(128)}) %tuple.65), condition=%wide.while_cond.9, body=%wide.while_body.9.sunk | while | flops 2 | bytes 2345 | solution.py:58
  51.5 5.3 gather_fusion.6
  62.6 9.6 %all-to-all-start.2 = ((bf16[16,64,128]{2,1,0:T(8,128)(2,1)}), bf16[16,64,128]{2,1,0:T(8,128)(2,1)S(1)}, u32[]{:S(2)}, u32[]{:S(2)}) async-start(bf16[16,64,128]{2,1,0:T(8,128)(2,1)} %bitcast_bitcast_fusion.2), calls=%async_computation.2 | async-start | bytes 524288 | tf_op jit(solution)/shard_map/all_to_all | solution.py:83
  74.2 12.8 %all-to-all-done.2 = bf16[16,64,128]{2,1,0:T(8,128)(2,1)S(1)} async-done(((bf16[16,64,128]{2,1,0:T(8,128)(2,1)}), bf16[16,64,128]{2,1,0:T(8,128)(2,1)S(1)}, u32[]{:S(2)}, u32[]{:S(2)}) %all-to-all-start.2) | async-done | bytes 262176 | tf_op jit(solution)/shard_map/all_to_all | solution.py:83
  87.0 3.5 all-to-all-start.4
  92.7 10.8 %all-to-all-done.4 = bf16[16,64,128]{2,1,0:T(8,128)(2,1)S(1)} async-done(((bf16[16,64,128]{2,1,0:T(8,128)(2,1)}), bf16[16,64,128]{2,1,0:T(8,128)(2,1)S(1)}, u32[]{:S(2)}, u32[]{:S(2)}) %all-to-all-start.4) | async-done | bytes 262176 | tf_op jit(solution)/shard_map/all_to_all | solution.py:84
  103.4 3.5 all-to-all-start.3
  110.7 8.3 %all-to-all-done.3 = bf16[16,64,128]{2,1,0:T(8,128)(2,1)S(1)} async-done(((bf16[16,64,128]{2,1,0:T(8,128)(2,1)}), bf16[16,64,128]{2,1,0:T(8,128)(2,1)S(1)}, u32[]{:S(2)}, u32[]{:S(2)}) %all-to-all-start.3) | async-done | bytes 262176 | tf_op jit(solution)/shard_map/all_to_all | solution.py:85
  119.0 3.5 all-to-all-start.1
  125.1 9.4 %all-to-all-done.1 = bf16[16,64,128]{2,1,0:T(8,128)(2,1)S(1)} async-done(((bf16[16,64,128]{2,1,0:T(8,128)(2,1)}), bf16[16,64,128]{2,1,0:T(8,128)(2,1)S(1)}, u32[]{:S(2)}, u32[]{:S(2)}) %all-to-all-start.1) | async-done | bytes 262176 | tf_op jit(solution)/shard_map/all_to_all | solution.py:81
  135.7 5.4 collective-permute-start.2
  143.7 6.0 collective-permute-start.3
  155.8 7.3 %all-to-all-start.5 = ((bf16[1,48,64,128]{3,2,0,1:T(8,128)(2,1)}), bf16[1,48,64,128]{3,2,0,1:T(8,128)(2,1)S(1)}, u32[]{:S(2)}, u32[]{:S(2)}) async-start(bf16[1,48,64,128]{3,2,0,1:T(8,128)(2,1)} %bitcast.32), calls=%async_computation.5 | async-start | bytes 1572864 | tf_op jit(solution)/shard_map/all_to_all | solution.py:168
  172.1 34.8 %all-reduce.9 = (f32[128]{0:T(128)S(1)}, f32[128]{0:T(128)S(1)}) all-reduce(f32[128]{0:T(128)S(1)} %copy-done.50, f32[128]{0:T(128)S(1)} %copy-done.52), channel_id=1, replica_groups=mesh['seq'=16,'head'=16] {'seq'}, use_global_device_ids=true, to_apply=%region_4.5 | all-reduce | flops 256 | bytes 2048 | tf_op jit(solution)/shard_map/psum | solution.py:15
  212.4 5.4 collective-permute-start.4
  220.5 3.9 collective-permute-start.7
  224.5 8.8 %all-to-all-start.6 = ((bf16[1,48,64,128]{3,2,0,1:T(8,128)(2,1)}), bf16[1,48,64,128]{3,2,0,1:T(8,128)(2,1)}, u32[]{:S(2)}, u32[]{:S(2)}) async-start(bf16[1,48,64,128]{3,2,0,1:T(8,128)(2,1)} %bitcast.35), calls=%async_computation.6 | async-start | bytes 1572864 | tf_op jit(solution)/shard_map/all_to_all | solution.py:169
  233.3 83.0 %all-reduce.17.cloned.1.call-done = (bf16[128,128]{1,0:T(8,128)(2,1)}, bf16[128,128]{1,0:T(8,128)(2,1)}, bf16[128,128]{1,0:T(8,128)(2,1)}, bf16[128,128]{1,0:T(8,128)(2,1)}) async-done(((bf16[128,128]{1,0:T(8,128)(2,1)}, bf16[128,128]{1,0:T(8,128)(2,1)}, bf16[128,128]{1,0:T(8,128)(2,1)}, bf16[128,128]{1,0:T(8,128)(2,1)}), (bf16[128,128]{1,0:T(8,128)(2,1)}, bf16[128,128]{1,0:T(8,128)(2,1)}, ...) | async-done | bytes 131088 | tf_op jit(solution)/shard_map/psum | solution.py:15
  326.8 14.7 %all-to-all-start.8 = ((f32[1,48,64,128]{3,2,0,1:T(8,128)}), f32[1,48,64,128]{3,2,0,1:T(8,128)}, u32[]{:S(2)}, u32[]{:S(2)}) async-start(f32[1,48,64,128]{3,2,0,1:T(8,128)} %multiply_bitcast_fusion), calls=%async_computation.8 | async-start | bytes 3145728 | tf_op jit(solution)/shard_map/all_to_all | solution.py:184
  351.7 140.2 %all-reduce.15.cloned.1.call-done = (bf16[1,128,128]{2,1,0:T(8,128)(2,1)}, bf16[1,128,128]{2,1,0:T(8,128)(2,1)}, bf16[1,128,128]{2,1,0:T(8,128)(2,1)}) async-done(((bf16[1,128,128]{2,1,0:T(8,128)(2,1)}, bf16[1,128,128]{2,1,0:T(8,128)(2,1)}, bf16[1,128,128]{2,1,0:T(8,128)(2,1)}), (bf16[1,128,128]{2,1,0:T(8,128)(2,1)}, bf16[1,128,128]{2,1,0:T(8,128)(2,1)}, ...) | async-done | bytes 98320 | tf_op jit(solution)/shard_map/psum | solution.py:151
  495.1 3.0 convolution_bitcast_fusion
  498.1 10.7 %all-to-all-start.10 = ((f32[1,48,64,128]{3,2,0,1:T(8,128)}), f32[1,48,64,128]{3,2,0,1:T(8,128)}, u32[]{:S(2)}, u32[]{:S(2)}) async-start(f32[1,48,64,128]{3,2,0,1:T(8,128)} %convolution_bitcast_fusion), calls=%async_computation.10 | async-start | bytes 3145728 | tf_op jit(solution)/shard_map/all_to_all | solution.py:185
  510.4 5.4 scatter_fusion
  520.1 5.4 scatter_fusion.1
  532.5 4.7 all-to-all-done.10
  537.2 9.0 %all-to-all-start.7 = ((bf16[16,2,4096]{2,1,0:T(2,128)(2,1)}), bf16[16,2,4096]{2,1,0:T(2,128)(2,1)S(1)}, u32[]{:S(2)}, u32[]{:S(2)}) async-start(bf16[16,2,4096]{2,1,0:T(2,128)(2,1)} %reshape.1101), calls=%async_computation.7 | async-start | bytes 524288 | tf_op jit(solution)/shard_map/all_to_all | solution.py:232
  546.2 5.4 scatter_fusion.2
  559.4 8.4 %all-to-all-start.11 = ((bf16[16,2,4096]{2,1,0:T(2,128)(2,1)}), bf16[16,2,4096]{2,1,0:T(2,128)(2,1)S(1)}, u32[]{:S(2)}, u32[]{:S(2)}) async-start(bf16[16,2,4096]{2,1,0:T(2,128)(2,1)} %reshape.1103), calls=%async_computation.11 | async-start | bytes 524288 | tf_op jit(solution)/shard_map/all_to_all | solution.py:242
  569.7 11.4 %all-to-all-done.11 = bf16[16,2,4096]{2,1,0:T(2,128)(2,1)S(1)} async-done(((bf16[16,2,4096]{2,1,0:T(2,128)(2,1)}), bf16[16,2,4096]{2,1,0:T(2,128)(2,1)S(1)}, u32[]{:S(2)}, u32[]{:S(2)}) %all-to-all-start.11) | async-done | bytes 262176 | tf_op jit(solution)/shard_map/all_to_all | solution.py:242
  581.1 3.5 all-to-all-start.9
  586.8 9.9 %all-to-all-done.9 = bf16[16,1,64,128]{3,2,1,0:T(8,128)(2,1)S(1)} async-done(((bf16[16,1,64,128]{3,2,1,0:T(8,128)(2,1)}), bf16[16,1,64,128]{3,2,1,0:T(8,128)(2,1)S(1)}, u32[]{:S(2)}, u32[]{:S(2)}) %all-to-all-start.9) | async-done | bytes 262176 | tf_op jit(solution)/shard_map/all_to_all | solution.py:234
  (334 shorter events, 126.6 us)
Async XLA Ops:
  8.9 53.7 %all-to-all-start = ((bf16[16,64,128]{2,1,0:T(8,128)(2,1)}), bf16[16,64,128]{2,1,0:T(8,128)(2,1)S(1)}, u32[]{:S(2)}, u32[]{:S(2)}) async-start(bf16[16,64,128]{2,1,0:T(8,128)(2,1)} %bitcast_bitcast_fusion.4), calls=%async_computation | async-start | bytes 524288 | tf_op jit(solution)/shard_map/all_to_all | solution.py:82
  56.8 34.3 %copy-start.27 = (bf16[64,2048]{1,0:T(8,128)(2,1)S(1)}, bf16[64,2048]{1,0:T(8,128)(2,1)}, u32[]{:S(2)}) copy-start(bf16[64,2048]{1,0:T(8,128)(2,1)} %param.25) | copy-start | bytes 786436
  56.9 35.1 %copy-start.28 = (bf16[64,2048]{1,0:T(8,128)(2,1)S(1)}, bf16[64,2048]{1,0:T(8,128)(2,1)}, u32[]{:S(2)}) copy-start(bf16[64,2048]{1,0:T(8,128)(2,1)} %param.29) | copy-start | bytes 786436
  60.5 62.4 %copy-start.39 = (s32[1024]{0:T(1024)}, s32[1024]{0:T(1024)S(1)}, u32[]{:S(2)}) copy-start(s32[1024]{0:T(1024)S(1)} %pad_clamp_fusion.1) | copy-start | bytes 12292
  62.6 24.4 %all-to-all-start.2 = ((bf16[16,64,128]{2,1,0:T(8,128)(2,1)}), bf16[16,64,128]{2,1,0:T(8,128)(2,1)S(1)}, u32[]{:S(2)}, u32[]{:S(2)}) async-start(bf16[16,64,128]{2,1,0:T(8,128)(2,1)} %bitcast_bitcast_fusion.2), calls=%async_computation.2 | async-start | bytes 524288 | tf_op jit(solution)/shard_map/all_to_all | solution.py:83
  87.0 16.4 %all-to-all-start.4 = ((bf16[16,64,128]{2,1,0:T(8,128)(2,1)}), bf16[16,64,128]{2,1,0:T(8,128)(2,1)S(1)}, u32[]{:S(2)}, u32[]{:S(2)}) async-start(bf16[16,64,128]{2,1,0:T(8,128)(2,1)} %bitcast_bitcast_fusion), calls=%async_computation.4 | async-start | bytes 524288 | tf_op jit(solution)/shard_map/all_to_all | solution.py:84
  103.4 15.6 %all-to-all-start.3 = ((bf16[16,64,128]{2,1,0:T(8,128)(2,1)}), bf16[16,64,128]{2,1,0:T(8,128)(2,1)S(1)}, u32[]{:S(2)}, u32[]{:S(2)}) async-start(bf16[16,64,128]{2,1,0:T(8,128)(2,1)} %bitcast_bitcast_fusion.1), calls=%async_computation.3 | async-start | bytes 524288 | tf_op jit(solution)/shard_map/all_to_all | solution.py:85
  119.0 15.5 %all-to-all-start.1 = ((bf16[16,64,128]{2,1,0:T(8,128)(2,1)}), bf16[16,64,128]{2,1,0:T(8,128)(2,1)S(1)}, u32[]{:S(2)}, u32[]{:S(2)}) async-start(bf16[16,64,128]{2,1,0:T(8,128)(2,1)} %bitcast_bitcast_fusion.3), calls=%async_computation.1 | async-start | bytes 524288 | tf_op jit(solution)/shard_map/all_to_all | solution.py:81
  135.7 71.3 %collective-permute-start.2 = (bf16[1,1,64,128]{3,2,1,0:T(8,128)(2,1)}, bf16[1,1,64,128]{3,2,1,0:T(8,128)(2,1)S(1)}, u32[]{:S(2)}, u32[]{:S(2)}) collective-permute-start(bf16[1,1,64,128]{3,2,1,0:T(8,128)(2,1)} %get-tuple-element.144), channel_id=1, source_target_pairs={{16,0},{32,16},{48,32},{64,48},{80,64},{96,80},{112,96},{128,112},... | collective-permute-start | bytes 49160 | tf_op jit(solution)/shard_map/ppermute | solution.py:21
  141.1 65.8 %collective-permute-start = (bf16[1,1,64,128]{3,2,1,0:T(8,128)(2,1)}, bf16[1,1,64,128]{3,2,1,0:T(8,128)(2,1)S(1)}, u32[]{:S(2)}, u32[]{:S(2)}) collective-permute-start(bf16[1,1,64,128]{3,2,1,0:T(8,128)(2,1)} %get-tuple-element.145), channel_id=1, source_target_pairs={{0,16},{16,32},{32,48},{48,64},{64,80},{80,96},{96,112},{112,128},... | collective-permute-start | bytes 49160 | tf_op jit(solution)/shard_map/ppermute | solution.py:21
  143.7 65.3 %collective-permute-start.3 = (bf16[1,1,64,128]{3,2,1,0:T(8,128)(2,1)S(1)}, bf16[1,1,64,128]{3,2,1,0:T(8,128)(2,1)S(1)}, u32[]{:S(2)}, u32[]{:S(2)}) collective-permute-start(bf16[1,1,64,128]{3,2,1,0:T(8,128)(2,1)S(1)} %get-tuple-element.142), channel_id=1, source_target_pairs={{16,0},{32,16},{48,32},{64,48},{80,64},{96,80},{112,96},{128,112},... | collective-permute-start | bytes 49160 | tf_op jit(solution)/shard_map/ppermute | solution.py:21
  149.7 58.3 %collective-permute-start.1 = (bf16[1,1,64,128]{3,2,1,0:T(8,128)(2,1)S(1)}, bf16[1,1,64,128]{3,2,1,0:T(8,128)(2,1)S(1)}, u32[]{:S(2)}, u32[]{:S(2)}) collective-permute-start(bf16[1,1,64,128]{3,2,1,0:T(8,128)(2,1)S(1)} %get-tuple-element.143), channel_id=1, source_target_pairs={{0,16},{16,32},{32,48},{48,64},{64,80},{80,96},{96,112},{112,128},... | collective-permute-start | bytes 49160 | tf_op jit(solution)/shard_map/ppermute | solution.py:21
  155.8 68.7 %all-to-all-start.5 = ((bf16[1,48,64,128]{3,2,0,1:T(8,128)(2,1)}), bf16[1,48,64,128]{3,2,0,1:T(8,128)(2,1)S(1)}, u32[]{:S(2)}, u32[]{:S(2)}) async-start(bf16[1,48,64,128]{3,2,0,1:T(8,128)(2,1)} %bitcast.32), calls=%async_computation.5 | async-start | bytes 1572864 | tf_op jit(solution)/shard_map/all_to_all | solution.py:168
  163.1 153.2 %all-reduce.17.cloned.1.call-start = ((), (), s32[]{:S(2)}) async-start(), calls=%async_computation.13 | async-start | bytes 262144 | tf_op jit(solution)/shard_map/psum | solution.py:15
  168.5 38.4 %copy-start.49 = (f32[64]{0:T(128)S(1)}, f32[64]{0:T(128)}, u32[]{:S(2)}) copy-start(f32[64]{0:T(128)} %get-tuple-element.153) | copy-start | bytes 772
  168.5 38.6 %copy-start.48 = (f32[64]{0:T(128)S(1)}, f32[64]{0:T(128)}, u32[]{:S(2)}) copy-start(f32[64]{0:T(128)} %get-tuple-element.152) | copy-start | bytes 772
  168.5 39.5 %copy-start.46 = (f32[64]{0:T(128)S(1)}, f32[64]{0:T(128)}, u32[]{:S(2)}) copy-start(f32[64]{0:T(128)} %get-tuple-element.151) | copy-start | bytes 772
  168.5 40.4 %copy-start.45 = (f32[64]{0:T(128)S(1)}, f32[64]{0:T(128)}, u32[]{:S(2)}) copy-start(f32[64]{0:T(128)} %get-tuple-element.150) | copy-start | bytes 772
  170.3 146.1 %copy-start.42 = (pred[1024]{0:T(1024)(128)(4,1)S(1)}, pred[1024]{0:T(1024)(128)(4,1)}, u32[]{:S(2)}) copy-start(pred[1024]{0:T(1024)(128)(4,1)} %broadcast_in_dim.110) | copy-start | bytes 3076
  206.9 110.4 %copy-start.37 = (bf16[1,1,64,128]{3,2,1,0:T(8,128)(2,1)}, bf16[1,1,64,128]{3,2,1,0:T(8,128)(2,1)S(1)}, u32[]{:S(2)}) copy-start(bf16[1,1,64,128]{3,2,1,0:T(8,128)(2,1)S(1)} %collective-permute-done) | copy-start | bytes 49156
  209.9 316.4 %collective-permute-start.5 = (bf16[1,1,64,128]{3,2,1,0:T(8,128)(2,1)}, bf16[1,1,64,128]{3,2,1,0:T(8,128)(2,1)}, u32[]{:S(2)}, u32[]{:S(2)}) collective-permute-start(bf16[1,1,64,128]{3,2,1,0:T(8,128)(2,1)} %fusion.58), channel_id=1, source_target_pairs={{0,16},{16,32},{32,48},{48,64},{64,80},{80,96},{96,112},{112,128},... | collective-permute-start | bytes 49160 | tf_op jit(solution)/shard_map/ppermute | solution.py:21
  212.4 313.1 %collective-permute-start.4 = (bf16[1,1,64,128]{3,2,1,0:T(8,128)(2,1)}, bf16[1,1,64,128]{3,2,1,0:T(8,128)(2,1)}, u32[]{:S(2)}, u32[]{:S(2)}) collective-permute-start(bf16[1,1,64,128]{3,2,1,0:T(8,128)(2,1)} %fusion.59), channel_id=1, source_target_pairs={{16,0},{32,16},{48,32},{64,48},{80,64},{96,80},{112,96},{128,112},... | collective-permute-start | bytes 49160 | tf_op jit(solution)/shard_map/ppermute | solution.py:21
  217.8 333.8 %collective-permute-start.6 = (bf16[1,1,64,128]{3,2,1,0:T(8,128)(2,1)}, bf16[1,1,64,128]{3,2,1,0:T(8,128)(2,1)}, u32[]{:S(2)}, u32[]{:S(2)}) collective-permute-start(bf16[1,1,64,128]{3,2,1,0:T(8,128)(2,1)} %fusion.56), channel_id=1, source_target_pairs={{16,0},{32,16},{48,32},{64,48},{80,64},{96,80},{112,96},{128,112},... | collective-permute-start | bytes 49160 | tf_op jit(solution)/shard_map/ppermute | solution.py:21
  220.5 332.4 %collective-permute-start.7 = (bf16[1,1,64,128]{3,2,1,0:T(8,128)(2,1)}, bf16[1,1,64,128]{3,2,1,0:T(8,128)(2,1)S(1)}, u32[]{:S(2)}, u32[]{:S(2)}) collective-permute-start(bf16[1,1,64,128]{3,2,1,0:T(8,128)(2,1)} %fusion.57), channel_id=1, source_target_pairs={{0,16},{16,32},{32,48},{48,64},{64,80},{80,96},{96,112},{112,128},... | collective-permute-start | bytes 49160 | tf_op jit(solution)/shard_map/ppermute | solution.py:21
  224.5 91.8 %copy-start.1 = (bf16[1,48,64,128]{3,2,0,1:T(8,128)(2,1)}, bf16[1,48,64,128]{3,2,0,1:T(8,128)(2,1)S(1)}, u32[]{:S(2)}) copy-start(bf16[1,48,64,128]{3,2,0,1:T(8,128)(2,1)S(1)} %all-to-all-done.5) | copy-start | bytes 2359300
  224.5 98.4 %all-to-all-start.6 = ((bf16[1,48,64,128]{3,2,0,1:T(8,128)(2,1)}), bf16[1,48,64,128]{3,2,0,1:T(8,128)(2,1)}, u32[]{:S(2)}, u32[]{:S(2)}) async-start(bf16[1,48,64,128]{3,2,0,1:T(8,128)(2,1)} %bitcast.35), calls=%async_computation.6 | async-start | bytes 1572864 | tf_op jit(solution)/shard_map/all_to_all | solution.py:169
  326.8 171.3 %all-to-all-start.8 = ((f32[1,48,64,128]{3,2,0,1:T(8,128)}), f32[1,48,64,128]{3,2,0,1:T(8,128)}, u32[]{:S(2)}, u32[]{:S(2)}) async-start(f32[1,48,64,128]{3,2,0,1:T(8,128)} %multiply_bitcast_fusion), calls=%async_computation.8 | async-start | bytes 3145728 | tf_op jit(solution)/shard_map/all_to_all | solution.py:184
  341.5 150.3 %all-reduce.15.cloned.1.call-start = ((), (), s32[]{:S(2)}) async-start(), calls=%async_computation.12 | async-start | bytes 196608 | tf_op jit(solution)/shard_map/psum | solution.py:151
  498.1 39.0 %all-to-all-start.10 = ((f32[1,48,64,128]{3,2,0,1:T(8,128)}), f32[1,48,64,128]{3,2,0,1:T(8,128)}, u32[]{:S(2)}, u32[]{:S(2)}) async-start(f32[1,48,64,128]{3,2,0,1:T(8,128)} %convolution_bitcast_fusion), calls=%async_computation.10 | async-start | bytes 3145728 | tf_op jit(solution)/shard_map/all_to_all | solution.py:185
  537.2 22.3 %all-to-all-start.7 = ((bf16[16,2,4096]{2,1,0:T(2,128)(2,1)}), bf16[16,2,4096]{2,1,0:T(2,128)(2,1)S(1)}, u32[]{:S(2)}, u32[]{:S(2)}) async-start(bf16[16,2,4096]{2,1,0:T(2,128)(2,1)} %reshape.1101), calls=%async_computation.7 | async-start | bytes 524288 | tf_op jit(solution)/shard_map/all_to_all | solution.py:232
  559.4 21.7 %all-to-all-start.11 = ((bf16[16,2,4096]{2,1,0:T(2,128)(2,1)}), bf16[16,2,4096]{2,1,0:T(2,128)(2,1)S(1)}, u32[]{:S(2)}, u32[]{:S(2)}) async-start(bf16[16,2,4096]{2,1,0:T(2,128)(2,1)} %reshape.1103), calls=%async_computation.11 | async-start | bytes 524288 | tf_op jit(solution)/shard_map/all_to_all | solution.py:242
  581.1 15.6 %all-to-all-start.9 = ((bf16[16,1,64,128]{3,2,1,0:T(8,128)(2,1)}), bf16[16,1,64,128]{3,2,1,0:T(8,128)(2,1)S(1)}, u32[]{:S(2)}, u32[]{:S(2)}) async-start(bf16[16,1,64,128]{3,2,1,0:T(8,128)(2,1)} %constant_dynamic-update-slice_fusion), calls=%async_computation.9 | async-start | bytes 524288 | tf_op jit(solution)/shard_map/all_to_all | solution.py:234
  (48 other events, 209.7 us)
Sparse Core Ops, SparseCore 0:
  167.8 148.4 all-reduce.16
  346.4 145.4 all-reduce.14
